TPU v7x, 512 devices: a whole 4x4x16 slice. The times are simulated.
512 devices in a mesh: pts: 16 (over z), elem: 32 (over y, x, core).
Axes of the slice: x: 4, y: 4, z: 16, core: 2. Of those that a mesh axis runs over, the one named last changes fastest.
Arguments:
- theta: float32 [1024, 1024], P('elem', 'pts'), may hold values from -3.140625 to 3.140625
- panel_rows: int32 [1024], P('elem'), may hold values from 0 to 1023, each once
- point_rows: int32 [32768], P('pts'), may hold values from 0 to 511
- point_cols: int32 [32768], P('pts'), may hold values from 0 to 255
- direct: float32 [2, 32768], P(None, 'pts'), may hold values from -3 to 3
- noise: float32 [32768], P('pts'), may hold values from 0.05 to 0.5
Outputs:
- phase_grad: float32 [1024, 1024], P('elem', 'pts')
- field: float32 [2, 32768], P(None, 'pts')
Inputs may be any that keep to these rules, and one draw needn't show every extreme that they name: `panel_rows`: each lattice row appears once.
All inputs are finite; a program needn't handle non-finite values.
Results may differ from a plain program's by a relative error of at most 0.0004.
Values sent between devices are 32-bit elements; how exact they have to be, the bound alone decides.
No kernel may reach another device: no remote copies, remote signals or barrier semaphores. Data moves between devices by JAX's collectives and lax.ppermute only.
A program may use at most 64 MiB of HBM per device.

v0:
```python
import math
import jax
import jax.numpy as jnp
from jax import lax
from jax.sharding import PartitionSpec as P

NX_EL = 1024
NY_EL = 1024
HIGH = lax.Precision.HIGHEST


def geometry(point_rows, point_cols):
    along_x = (point_rows.astype(jnp.float32) - 255.5) * 0.5
    along_y = (point_cols.astype(jnp.float32) - 127.5) * 0.5
    radius = jnp.sqrt(along_x * along_x + along_y * along_y + 1600.0)
    return (along_x / radius, along_y / radius, 80.0 / (radius * math.sqrt(NX_EL * NY_EL)))


def partial_field(slope_x, slope_y, lattice_x, lattice_y, phase_re, phase_im):
    beam_y = math.pi * slope_y[:, None] * lattice_y[None, :]
    left = jnp.concatenate([jnp.cos(beam_y), jnp.sin(beam_y)], 1)
    right = jnp.concatenate(
        [
            jnp.concatenate([phase_re.T, phase_im.T], 1),
            jnp.concatenate([-phase_im.T, phase_re.T], 1),
        ],
        0,
    )
    inner = jnp.dot(left, right, precision=HIGH, preferred_element_type=jnp.float32)
    width = phase_re.shape[0]
    inner_re = inner[:, :width]
    inner_im = inner[:, width:]
    beam_x = math.pi * slope_x[:, None] * lattice_x[None, :]
    cos_x = jnp.cos(beam_x)
    sin_x = jnp.sin(beam_x)
    return jnp.stack(
        [
            jnp.sum(cos_x * inner_re - sin_x * inner_im, 1),
            jnp.sum(cos_x * inner_im + sin_x * inner_re, 1),
        ]
    )


def surface_terms(slope_x, slope_y, q_re, q_im, lattice_x, lattice_y):
    beam_x = math.pi * slope_x[:, None] * lattice_x[None, :]
    cos_x = jnp.cos(beam_x)
    sin_x = jnp.sin(beam_x)
    weight_re = q_re[:, None] * cos_x - q_im[:, None] * sin_x
    weight_im = q_re[:, None] * sin_x + q_im[:, None] * cos_x
    beam_y = math.pi * slope_y[:, None] * lattice_y[None, :]
    left = jnp.concatenate([jnp.cos(beam_y), jnp.sin(beam_y)], 1)
    right = jnp.concatenate([weight_re, weight_im], 1)
    prod = lax.dot_general(
        left, right, (((0,), (0,)), ((), ())), precision=HIGH, preferred_element_type=jnp.float32
    )
    rows_y = lattice_y.shape[0]
    cols_x = lattice_x.shape[0]
    sum_re = prod[:rows_y, :cols_x] - prod[rows_y:, cols_x:]
    sum_im = prod[:rows_y, cols_x:] + prod[rows_y:, :cols_x]
    return jnp.concatenate([sum_re, sum_im], 1)


def block_size(points, cols_y):
    return math.gcd(points, min(points, max(256, 524288 // cols_y)))


def field_blocks(slope_x, slope_y, lattice_x, lattice_y, phase_re, phase_im):
    block = block_size(slope_x.shape[0], lattice_y.shape[0])
    count = slope_x.shape[0] // block

    def one_block(pair):
        return partial_field(pair[0], pair[1], lattice_x, lattice_y, phase_re, phase_im)

    parts = lax.map(one_block, (slope_x.reshape(count, block), slope_y.reshape(count, block)))
    return jnp.transpose(parts, (1, 0, 2)).reshape(2, count * block)


def terms_blocks(slope_x, slope_y, q_re, q_im, lattice_x, lattice_y):
    block = block_size(slope_x.shape[0], lattice_y.shape[0])
    count = slope_x.shape[0] // block
    start = jnp.zeros((lattice_y.shape[0], 2 * lattice_x.shape[0]), jnp.float32)

    def step(carry, items):
        return (
            carry + surface_terms(items[0], items[1], items[2], items[3], lattice_x, lattice_y),
            None,
        )

    items = (
        slope_x.reshape(count, block),
        slope_y.reshape(count, block),
        q_re.reshape(count, block),
        q_im.reshape(count, block),
    )
    total, unused = lax.scan(step, start, items)
    return total


def weights(field, scale, noise):
    power = noise + field[0] * field[0] + field[1] * field[1]
    return (field[0] * scale / power, -field[1] * scale / power)


def gradient(terms, phase_re, phase_im):
    cols_x = phase_re.shape[0]
    sum_re = terms[:, :cols_x].T
    sum_im = terms[:, cols_x:].T
    return -2.0 * (phase_re * sum_im + phase_im * sum_re)


def shards(theta, panel_rows, point_rows, point_cols, direct, noise):
    slope_x, slope_y, scale = geometry(point_rows, point_cols)
    phase_re = jnp.cos(theta)
    phase_im = jnp.sin(theta)
    lattice_x = panel_rows.astype(jnp.float32) - (NX_EL - 1) / 2.0
    cols_dev = theta.shape[1]
    phasors = jnp.stack([phase_re, phase_im])
    whole = lax.all_gather(phasors, "pts", axis=2, tiled=True)
    lattice_y = jnp.arange(NY_EL).astype(jnp.float32) - (NY_EL - 1) / 2.0
    partial_value = field_blocks(slope_x, slope_y, lattice_x, lattice_y, whole[0], whole[1])
    total = lax.psum(partial_value, "elem")
    field = direct + scale[None, :] * total
    q_re, q_im = weights(field, scale, noise)
    cols_here = jnp.arange(cols_dev * lax.axis_size("pts")).astype(jnp.float32) - (NY_EL - 1) / 2.0
    terms = lax.psum_scatter(
        terms_blocks(slope_x, slope_y, q_re, q_im, lattice_x, cols_here),
        "pts",
        scatter_dimension=0,
        tiled=True,
    )
    return (gradient(terms, phase_re, phase_im), field)


def solution(mesh):
    in_specs = (P("elem", "pts"), P("elem"), P("pts"), P("pts"), P(None, "pts"), P("pts"))
    out_specs = (P("elem", "pts"), P(None, "pts"))
    return jax.shard_map(shards, mesh=mesh, in_specs=in_specs, out_specs=out_specs, check_vma=False)
```

profile of v0, /device:TPU:2, one launch (start us, length us, event | category | flops | bytes accessed | tf_op | source)
XLA Modules:
  0.0 337.5 jit_solution(4195258781509086454)
XLA Ops:
  7.2 0.8 copy.18
  8.3 41.7 %all_gather.3 = f32[2,32,1024]{1,0,2:T(2,128)S(1)} all-gather(f32[2,32,64]{1,0,2:T(2,128)S(1)} %pad_maximum_fusion), channel_id=1, replica_groups=mesh['pts'=16,'elem'=32] {'pts'}, dimensions={2}, use_global_device_ids=true | all-gather | bytes 278528 | tf_op jit(solution)/shard_map/all_gather | solution.py:118
  49.9 0.8 fusion.38
  50.9 0.3 maximum_maximum_fusion
  51.3 47.9 %while.24 = (s32[]{:T(128)}, f32[4,2,512]{2,1,0:T(2,128)S(1)}, f32[4,512]{1,0:T(4,128)S(1)}, f32[32]{0:T(128)S(1)}, f32[4,512]{1,0:T(4,128)S(1)}, /*index=5*/f32[2048,64]{1,0:T(8,128)S(1)}, s32[]{:T(128)}) while((s32[]{:T(128)}, f32[4,2,512]{2,1,0:T(2,128)S(1)}, f32[4,512]{1,0:T(4,128)S(1)}, f32[32]{0:T(128)S(1)}, ...), condition=%wide.region_3.4_spmd.clone, body=%wide.region_0.3_spmd.clone.sunk | while | flops 807029760 | bytes 9208021 | solution.py:74
  51.3 7.3 %multiply_cosine_fusion.6 = (f32[512,1024]{1,0:T(8,128)S(1)}, f32[512,1024]{1,0:T(8,128)S(1)}) fusion(f32[1024]{0:T(1024)S(1)} %convert_add_fusion.5, f32[512]{0:T(512)S(1)} %bitcast.76), kind=kLoop, calls=%fused_computation.7.clone.1 | loop fusion | flops 524288 | bytes 4200448 | tf_op jit(solution)/shard_map/while/body/eval_jaxpr/cos | solution.py:21
  58.7 4.2 %fusion.52 = f32[512,64]{0,1:T(8,128)S(1)} fusion(f32[2048,64]{1,0:T(8,128)S(1)} %get-tuple-element.375, f32[512,1024]{1,0:T(8,128)S(1)} %get-tuple-element.334, f32[512,1024]{1,0:T(8,128)S(1)} %get-tuple-element.335), kind=kOutput, calls=%fused_computation.2.clone.1 | convolution fusion | flops 806354944 | bytes 4849664 | tf_op jit(solution)/shard_map/while/body/eval_jaxpr/dot_general | solution.py:29
  62.9 0.3 fusion.53
  63.3 7.3 %multiply_cosine_fusion.6 = (f32[512,1024]{1,0:T(8,128)S(1)}, f32[512,1024]{1,0:T(8,128)S(1)}) fusion(f32[1024]{0:T(1024)S(1)} %convert_add_fusion.5, f32[512]{0:T(512)S(1)} %bitcast.76), kind=kLoop, calls=%fused_computation.7.clone.1 | loop fusion | flops 524288 | bytes 4200448 | tf_op jit(solution)/shard_map/while/body/eval_jaxpr/cos | solution.py:21
  70.6 4.2 %fusion.52 = f32[512,64]{0,1:T(8,128)S(1)} fusion(f32[2048,64]{1,0:T(8,128)S(1)} %get-tuple-element.375, f32[512,1024]{1,0:T(8,128)S(1)} %get-tuple-element.334, f32[512,1024]{1,0:T(8,128)S(1)} %get-tuple-element.335), kind=kOutput, calls=%fused_computation.2.clone.1 | convolution fusion | flops 806354944 | bytes 4849664 | tf_op jit(solution)/shard_map/while/body/eval_jaxpr/dot_general | solution.py:29
  74.9 0.3 fusion.53
  75.3 7.3 %multiply_cosine_fusion.6 = (f32[512,1024]{1,0:T(8,128)S(1)}, f32[512,1024]{1,0:T(8,128)S(1)}) fusion(f32[1024]{0:T(1024)S(1)} %convert_add_fusion.5, f32[512]{0:T(512)S(1)} %bitcast.76), kind=kLoop, calls=%fused_computation.7.clone.1 | loop fusion | flops 524288 | bytes 4200448 | tf_op jit(solution)/shard_map/while/body/eval_jaxpr/cos | solution.py:21
  82.6 4.2 %fusion.52 = f32[512,64]{0,1:T(8,128)S(1)} fusion(f32[2048,64]{1,0:T(8,128)S(1)} %get-tuple-element.375, f32[512,1024]{1,0:T(8,128)S(1)} %get-tuple-element.334, f32[512,1024]{1,0:T(8,128)S(1)} %get-tuple-element.335), kind=kOutput, calls=%fused_computation.2.clone.1 | convolution fusion | flops 806354944 | bytes 4849664 | tf_op jit(solution)/shard_map/while/body/eval_jaxpr/dot_general | solution.py:29
  86.8 0.3 fusion.53
  87.2 7.3 %multiply_cosine_fusion.6 = (f32[512,1024]{1,0:T(8,128)S(1)}, f32[512,1024]{1,0:T(8,128)S(1)}) fusion(f32[1024]{0:T(1024)S(1)} %convert_add_fusion.5, f32[512]{0:T(512)S(1)} %bitcast.76), kind=kLoop, calls=%fused_computation.7.clone.1 | loop fusion | flops 524288 | bytes 4200448 | tf_op jit(solution)/shard_map/while/body/eval_jaxpr/cos | solution.py:21
  94.6 4.2 %fusion.52 = f32[512,64]{0,1:T(8,128)S(1)} fusion(f32[2048,64]{1,0:T(8,128)S(1)} %get-tuple-element.375, f32[512,1024]{1,0:T(8,128)S(1)} %get-tuple-element.334, f32[512,1024]{1,0:T(8,128)S(1)} %get-tuple-element.335), kind=kOutput, calls=%fused_computation.2.clone.1 | convolution fusion | flops 806354944 | bytes 4849664 | tf_op jit(solution)/shard_map/while/body/eval_jaxpr/dot_general | solution.py:29
  98.8 0.3 fusion.53
  99.2 119.2 %psum.7 = f32[2,2048]{1,0:T(2,128)S(1)} all-reduce(f32[2,2048]{1,0:T(2,128)S(1)} %bitcast.82), channel_id=1, replica_groups=mesh['pts'=16,'elem'=32] {'elem'}, use_global_device_ids=true, to_apply=%region_4.5 | all-reduce | flops 4096 | bytes 32768 | tf_op jit(solution)/shard_map/psum | solution.py:121
  218.4 0.5 copy-done
  219.0 42.9 %while.25 = (s32[]{:T(128)}, f32[1024,64]{0,1:T(8,128)S(1)}, f32[4,512]{1,0:T(4,128)S(1)}, f32[4,512]{1,0:T(4,128)S(1)}, f32[4,512]{1,0:T(4,128)S(1)}, /*index=5...) while((s32[]{:T(128)}, f32[1024,64]{0,1:T(8,128)S(1)}, f32[4,512]{1,0:T(4,128)S(1)}, ...), condition=%wide.region_6.7_spmd.clone, body=%wide.region_5.6_spmd.clone.sunk | while | flops 807291904 | bytes 10780911 | solution.py:95
  219.3 7.3 %multiply_cosine_fusion.7 = (f32[512,1024]{1,0:T(8,128)S(1)}, f32[512,1024]{1,0:T(8,128)S(1)}) fusion(f32[1024]{0:T(1024)S(1)} %convert_add_fusion.6, f32[512]{0:T(512)S(1)} %bitcast.72), kind=kLoop, calls=%fused_computation.29.clone.1 | loop fusion | flops 524288 | bytes 4200448 | tf_op jit(solution)/shard_map/while/body/eval_jaxpr/cos | solution.py:51
  226.7 2.8 fusion.58
  230.1 7.3 %multiply_cosine_fusion.7 = (f32[512,1024]{1,0:T(8,128)S(1)}, f32[512,1024]{1,0:T(8,128)S(1)}) fusion(f32[1024]{0:T(1024)S(1)} %convert_add_fusion.6, f32[512]{0:T(512)S(1)} %bitcast.72), kind=kLoop, calls=%fused_computation.29.clone.1 | loop fusion | flops 524288 | bytes 4200448 | tf_op jit(solution)/shard_map/while/body/eval_jaxpr/cos | solution.py:51
  237.4 2.8 fusion.58
  240.8 7.3 %multiply_cosine_fusion.7 = (f32[512,1024]{1,0:T(8,128)S(1)}, f32[512,1024]{1,0:T(8,128)S(1)}) fusion(f32[1024]{0:T(1024)S(1)} %convert_add_fusion.6, f32[512]{0:T(512)S(1)} %bitcast.72), kind=kLoop, calls=%fused_computation.29.clone.1 | loop fusion | flops 524288 | bytes 4200448 | tf_op jit(solution)/shard_map/while/body/eval_jaxpr/cos | solution.py:51
  248.1 2.8 fusion.58
  251.5 7.3 %multiply_cosine_fusion.7 = (f32[512,1024]{1,0:T(8,128)S(1)}, f32[512,1024]{1,0:T(8,128)S(1)}) fusion(f32[1024]{0:T(1024)S(1)} %convert_add_fusion.6, f32[512]{0:T(512)S(1)} %bitcast.72), kind=kLoop, calls=%fused_computation.29.clone.1 | loop fusion | flops 524288 | bytes 4200448 | tf_op jit(solution)/shard_map/while/body/eval_jaxpr/cos | solution.py:51
  258.8 2.8 fusion.58
  261.8 1.0 copy.26
  262.9 66.2 %reduce-scatter.4.cloned.1.call-done = f32[64,64]{1,0:T(8,128)} async-done(((f32[1024,64]{1,0:T(8,128)}), f32[64,64]{1,0:T(8,128)}) %reduce-scatter.4.cloned.1.call-update) | async-done | bytes 16400 | tf_op jit(solution)/shard_map/reduce_scatter | solution.py:125
  329.1 0.9 fusion.34
  330.0 0.7 copy.25
  (63 shorter events, 2.4 us)
Async XLA Ops:
  7.2 321.9 %reduce-scatter.4.cloned.1.call-start = ((), (), s32[]{:S(2)}) async-start(), calls=%async_computation.1 | async-start | bytes 557056 | tf_op jit(solution)/shard_map/reduce_scatter | solution.py:125
  8.2 42.6 %copy-start.2 = (s32[2048]{0:T(1024)S(1)}, s32[2048]{0:T(1024)}, u32[]{:S(2)}) copy-start(s32[2048]{0:T(1024)} %param.13) | copy-start | bytes 24580
  8.3 42.6 %copy-start.3 = (s32[2048]{0:T(1024)S(1)}, s32[2048]{0:T(1024)}, u32[]{:S(2)}) copy-start(s32[2048]{0:T(1024)} %param.12) | copy-start | bytes 24580
  8.3 42.6 %copy-start.5 = (s32[32]{0:T(128)S(1)}, s32[32]{0:T(128)}, u32[]{:S(2)}) copy-start(s32[32]{0:T(128)} %param.11) | copy-start | bytes 388
  51.2 167.1 %copy-start.1 = (f32[2,2048]{1,0:T(2,128)S(1)}, f32[2,2048]{1,0:T(2,128)}, u32[]{:S(2)}) copy-start(f32[2,2048]{1,0:T(2,128)} %param.14) | copy-start | bytes 49156
  51.3 167.1 %copy-start.4 = (f32[2048]{0:T(1024)S(1)}, f32[2048]{0:T(1024)}, u32[]{:S(2)}) copy-start(f32[2048]{0:T(1024)} %param.15) | copy-start | bytes 24580
  218.4 0.6 copy-start
Sparse Core Ops, SparseCore 0:
  263.0 66.0 reduce-scatter.3
where the time goes:
time: 338 us
  blocking collectives  161 us (48%)
  waiting for transfers between devices  66.2 us (20%)
  other arithmetic  63.5 us (19%)
  matrix products  28.3 us (8%)
  between operations  14.2 us (4%)
  local copies, waits for them, and re-layouts  4.05 us (1%)
    psum x1, blocking collectives, shards(): total = lax.psum(partial_value, 'elem')  119 us
    reduce_scatter x1, waiting for transfers between devices, shards(): lax.psum_scatter(terms_blocks(slope_x, slope_y, q_re, q_im, lattice_x, co...  66.2 us
    all_gather x1, blocking collectives, shards(): whole = lax.all_gather(phasors, 'pts', axis=2, tiled=True)  41.7 us
    cos x4, other arithmetic, partial_field(): left = jnp.concatenate([jnp.cos(beam_y), jnp.sin(beam_y)], 1)  29.4 us
    cos x4, other arithmetic, surface_terms(): left = jnp.concatenate([jnp.cos(beam_y), jnp.sin(beam_y)], 1)  29.4 us
    dot_general x4, matrix products, partial_field(): jnp.dot(left, right, precision=HIGH, preferred_element_type=jnp.float32)  16.9 us
    dot_general x4, matrix products, surface_terms(): lax.dot_general(left, right, (((0,), (0,)), ((), ())), precision=HIGH, pr...  11.4 us
  transfers between devices with their start and end apart: 1, of which 1 were waited for; matrix products, arithmetic and copies ran while one was open for 0% of the time, Pallas kernels for 0%

commit v1 on v0

--- a/solution.py
+++ b/solution.py
@@ -1,3 +1,4 @@
+import functools
 import math
 import jax
 import jax.numpy as jnp
@@ -7,6 +8,18 @@
 NX_EL = 1024
 NY_EL = 1024
 HIGH = lax.Precision.HIGHEST
+
+
+def derive_bands(z_in, mesh_ax):
+    how_many = lax.axis_size(mesh_ax)
+    current_block = lambda piece_now: [(j, j ^ piece_now) for j in range(how_many)]
+    near = z_in
+    for i in range(how_many.bit_length() - 1):
+        near = near + lax.ppermute(near, mesh_ax, current_block(1 << i))
+    return near
+
+
+work_columns = functools.partial(derive_bands, mesh_ax="elem")
 
 
 def geometry(point_rows, point_cols):
@@ -118,7 +131,7 @@
     whole = lax.all_gather(phasors, "pts", axis=2, tiled=True)
     lattice_y = jnp.arange(NY_EL).astype(jnp.float32) - (NY_EL - 1) / 2.0
     partial_value = field_blocks(slope_x, slope_y, lattice_x, lattice_y, whole[0], whole[1])
-    total = lax.psum(partial_value, "elem")
+    total = work_columns(partial_value)
     field = direct + scale[None, :] * total
     q_re, q_im = weights(field, scale, noise)
     cols_here = jnp.arange(cols_dev * lax.axis_size("pts")).astype(jnp.float32) - (NY_EL - 1) / 2.0

time: 338 us -> 247 us (0.73)
  blocking collectives: 161 us -> 41.7 us
  starting transfers between devices: 0.04 us -> 17 us
  waiting for transfers between devices: 66.2 us -> 77.9 us
    psum x1 -> x0, blocking collectives: 119 us -> none  [shards(): total = lax.psum(partial_value, 'elem')]
    ppermute x0 -> x5, starting transfers between devices: none -> 17 us  [derive_bands(): near = near + lax.ppermute(near, mesh_ax, current_block(1 << i))]
    ppermute x0 -> x5, waiting for transfers between devices: none -> 11.6 us  [derive_bands(): near = near + lax.ppermute(near, mesh_ax, current_block(1 << i))]
  transfers between devices with their start and end apart: 1 -> 6, of which waited for: 1 -> 6; matrix products, arithmetic and copies ran while one was open for 0% -> 0% of each run, Pallas kernels for 0% -> 0%
where the time goes in v1:
time: 247 us
  waiting for transfers between devices  77.9 us (32%)
  other arithmetic  63.5 us (26%)
  blocking collectives  41.7 us (17%)
  matrix products  28.3 us (11%)
  starting transfers between devices  17 us (7%)
  between operations  14.3 us (6%)
  local copies, waits for them, and re-layouts  4.04 us (2%)
    reduce_scatter x1, waiting for transfers between devices, shards(): lax.psum_scatter(terms_blocks(slope_x, slope_y, q_re, q_im, lattice_x, co...  66.3 us
    all_gather x1, blocking collectives, shards(): whole = lax.all_gather(phasors, 'pts', axis=2, tiled=True)  41.7 us
    cos x4, other arithmetic, surface_terms(): left = jnp.concatenate([jnp.cos(beam_y), jnp.sin(beam_y)], 1)  29.4 us
    cos x4, other arithmetic, partial_field(): left = jnp.concatenate([jnp.cos(beam_y), jnp.sin(beam_y)], 1)  29.4 us
    ppermute x5, starting transfers between devices, derive_bands(): near = near + lax.ppermute(near, mesh_ax, current_block(1 << i))  17 us
    dot_general x4, matrix products, partial_field(): jnp.dot(left, right, precision=HIGH, preferred_element_type=jnp.float32)  16.9 us
    ppermute x5, waiting for transfers between devices, derive_bands(): near = near + lax.ppermute(near, mesh_ax, current_block(1 << i))  11.6 us
    dot_general x4, matrix products, surface_terms(): lax.dot_general(left, right, (((0,), (0,)), ((), ())), precision=HIGH, pr...  11.4 us
  transfers between devices with their start and end apart: 6, of which 6 were waited for; matrix products, arithmetic and copies ran while one was open for 0% of the time, Pallas kernels for 0%

profile of v1, /device:TPU:2, one launch (start us, length us, event | category | flops | bytes accessed | tf_op | source)
XLA Modules:
  0.0 247.1 jit_solution(7936981296764045781)
XLA Ops:
  8.3 41.7 %all_gather.3 = f32[2,32,1024]{1,0,2:T(2,128)S(1)} all-gather(f32[2,32,64]{1,0,2:T(2,128)S(1)} %pad_maximum_fusion), channel_id=1, replica_groups=mesh['pts'=16,'elem'=32] {'pts'}, dimensions={2}, use_global_device_ids=true | all-gather | bytes 278528 | tf_op jit(solution)/shard_map/all_gather | solution.py:131
  51.3 47.9 %while.24 = (s32[]{:T(128)}, f32[4,2,512]{2,1,0:T(2,128)S(1)}, f32[4,512]{1,0:T(4,128)S(1)}, f32[32]{0:T(128)S(1)}, f32[4,512]{1,0:T(4,128)S(1)}, /*index=5*/f32[2048,64]{1,0:T(8,128)S(1)}, s32[]{:T(128)}) while((s32[]{:T(128)}, f32[4,2,512]{2,1,0:T(2,128)S(1)}, f32[4,512]{1,0:T(4,128)S(1)}, f32[32]{0:T(128)S(1)}, ...), condition=%wide.region_3.4_spmd.clone, body=%wide.region_0.3_spmd.clone.sunk | while | flops 807029760 | bytes 9208021 | solution.py:87
  51.3 7.3 %multiply_cosine_fusion.6 = (f32[512,1024]{1,0:T(8,128)S(1)}, f32[512,1024]{1,0:T(8,128)S(1)}) fusion(f32[1024]{0:T(1024)S(1)} %convert_add_fusion.5, f32[512]{0:T(512)S(1)} %bitcast.76), kind=kLoop, calls=%fused_computation.7.clone.1 | loop fusion | flops 524288 | bytes 4200448 | tf_op jit(solution)/shard_map/while/body/eval_jaxpr/cos | solution.py:34
  58.7 4.2 %fusion.52 = f32[512,64]{0,1:T(8,128)S(1)} fusion(f32[2048,64]{1,0:T(8,128)S(1)} %get-tuple-element.375, f32[512,1024]{1,0:T(8,128)S(1)} %get-tuple-element.334, f32[512,1024]{1,0:T(8,128)S(1)} %get-tuple-element.335), kind=kOutput, calls=%fused_computation.2.clone.1 | convolution fusion | flops 806354944 | bytes 4849664 | tf_op jit(solution)/shard_map/while/body/eval_jaxpr/dot_general | solution.py:42
  63.3 7.3 %multiply_cosine_fusion.6 = (f32[512,1024]{1,0:T(8,128)S(1)}, f32[512,1024]{1,0:T(8,128)S(1)}) fusion(f32[1024]{0:T(1024)S(1)} %convert_add_fusion.5, f32[512]{0:T(512)S(1)} %bitcast.76), kind=kLoop, calls=%fused_computation.7.clone.1 | loop fusion | flops 524288 | bytes 4200448 | tf_op jit(solution)/shard_map/while/body/eval_jaxpr/cos | solution.py:34
  70.6 4.2 %fusion.52 = f32[512,64]{0,1:T(8,128)S(1)} fusion(f32[2048,64]{1,0:T(8,128)S(1)} %get-tuple-element.375, f32[512,1024]{1,0:T(8,128)S(1)} %get-tuple-element.334, f32[512,1024]{1,0:T(8,128)S(1)} %get-tuple-element.335), kind=kOutput, calls=%fused_computation.2.clone.1 | convolution fusion | flops 806354944 | bytes 4849664 | tf_op jit(solution)/shard_map/while/body/eval_jaxpr/dot_general | solution.py:42
  75.2 7.3 %multiply_cosine_fusion.6 = (f32[512,1024]{1,0:T(8,128)S(1)}, f32[512,1024]{1,0:T(8,128)S(1)}) fusion(f32[1024]{0:T(1024)S(1)} %convert_add_fusion.5, f32[512]{0:T(512)S(1)} %bitcast.76), kind=kLoop, calls=%fused_computation.7.clone.1 | loop fusion | flops 524288 | bytes 4200448 | tf_op jit(solution)/shard_map/while/body/eval_jaxpr/cos | solution.py:34
  82.6 4.2 %fusion.52 = f32[512,64]{0,1:T(8,128)S(1)} fusion(f32[2048,64]{1,0:T(8,128)S(1)} %get-tuple-element.375, f32[512,1024]{1,0:T(8,128)S(1)} %get-tuple-element.334, f32[512,1024]{1,0:T(8,128)S(1)} %get-tuple-element.335), kind=kOutput, calls=%fused_computation.2.clone.1 | convolution fusion | flops 806354944 | bytes 4849664 | tf_op jit(solution)/shard_map/while/body/eval_jaxpr/dot_general | solution.py:42
  87.2 7.3 %multiply_cosine_fusion.6 = (f32[512,1024]{1,0:T(8,128)S(1)}, f32[512,1024]{1,0:T(8,128)S(1)}) fusion(f32[1024]{0:T(1024)S(1)} %convert_add_fusion.5, f32[512]{0:T(512)S(1)} %bitcast.76), kind=kLoop, calls=%fused_computation.7.clone.1 | loop fusion | flops 524288 | bytes 4200448 | tf_op jit(solution)/shard_map/while/body/eval_jaxpr/cos | solution.py:34
  94.6 4.2 %fusion.52 = f32[512,64]{0,1:T(8,128)S(1)} fusion(f32[2048,64]{1,0:T(8,128)S(1)} %get-tuple-element.375, f32[512,1024]{1,0:T(8,128)S(1)} %get-tuple-element.334, f32[512,1024]{1,0:T(8,128)S(1)} %get-tuple-element.335), kind=kOutput, calls=%fused_computation.2.clone.1 | convolution fusion | flops 806354944 | bytes 4849664 | tf_op jit(solution)/shard_map/while/body/eval_jaxpr/dot_general | solution.py:42
  99.2 1.9 collective-permute-start
  101.1 1.1 collective-permute-done
  102.3 2.4 collective-permute-start.1
  104.7 3.2 %collective-permute-done.1 = f32[2,2048]{1,0:T(2,128)S(1)} collective-permute-done((f32[2,2048]{1,0:T(2,128)S(1)}, f32[2,2048]{1,0:T(2,128)S(1)}, u32[]{:S(2)}, u32[]{:S(2)}) %collective-permute-start.1) | collective-permute-done | bytes 16416 | tf_op jit(solution)/shard_map/ppermute | solution.py:18
  107.9 4.0 %collective-permute-start.2 = (f32[2,2048]{1,0:T(2,128)S(1)}, f32[2,2048]{1,0:T(2,128)S(1)}, u32[]{:S(2)}, u32[]{:S(2)}) collective-permute-start(f32[2,2048]{1,0:T(2,128)S(1)} %add.68), channel_id=1, source_target_pairs={{0,4},{1,5},{2,6},{3,7},{4,0},{5,1},{6,2},{7,3},{8,12},{9,13},{10,... | collective-permute-start | bytes 49160 | tf_op jit(solution)/shard_map/ppermute | solution.py:18
  111.9 3.1 %collective-permute-done.2 = f32[2,2048]{1,0:T(2,128)S(1)} collective-permute-done((f32[2,2048]{1,0:T(2,128)S(1)}, f32[2,2048]{1,0:T(2,128)S(1)}, u32[]{:S(2)}, u32[]{:S(2)}) %collective-permute-start.2) | collective-permute-done | bytes 16416 | tf_op jit(solution)/shard_map/ppermute | solution.py:18
  115.1 3.5 %collective-permute-start.3 = (f32[2,2048]{1,0:T(2,128)S(1)}, f32[2,2048]{1,0:T(2,128)S(1)}, u32[]{:S(2)}, u32[]{:S(2)}) collective-permute-start(f32[2,2048]{1,0:T(2,128)S(1)} %add.69), channel_id=1, source_target_pairs={{0,8},{1,9},{2,10},{3,11},{4,12},{5,13},{6,14},{7,15},{8,0},{9,1},... | collective-permute-start | bytes 49160 | tf_op jit(solution)/shard_map/ppermute | solution.py:18
  118.5 2.1 collective-permute-done.3
  120.7 5.1 %collective-permute-start.4 = (f32[2,2048]{1,0:T(2,128)S(1)}, f32[2,2048]{1,0:T(2,128)S(1)}, u32[]{:S(2)}, u32[]{:S(2)}) collective-permute-start(f32[2,2048]{1,0:T(2,128)S(1)} %add.70), channel_id=1, source_target_pairs={{0,16},{1,17},{2,18},{3,19},{4,20},{5,21},{6,22},{7,23},{8,24},{9,... | collective-permute-start | bytes 49160 | tf_op jit(solution)/shard_map/ppermute | solution.py:18
  125.8 2.0 collective-permute-done.4
  128.5 42.9 %while.25 = (s32[]{:T(128)}, f32[1024,64]{0,1:T(8,128)S(1)}, f32[4,512]{1,0:T(4,128)S(1)}, f32[4,512]{1,0:T(4,128)S(1)}, f32[4,512]{1,0:T(4,128)S(1)}, /*index=5...) while((s32[]{:T(128)}, f32[1024,64]{0,1:T(8,128)S(1)}, f32[4,512]{1,0:T(4,128)S(1)}, ...), condition=%wide.region_5.6_spmd.clone, body=%wide.region_4.5_spmd.clone.sunk | while | flops 807291904 | bytes 10780911 | solution.py:108
  128.8 7.3 %multiply_cosine_fusion.7 = (f32[512,1024]{1,0:T(8,128)S(1)}, f32[512,1024]{1,0:T(8,128)S(1)}) fusion(f32[1024]{0:T(1024)S(1)} %convert_add_fusion.6, f32[512]{0:T(512)S(1)} %bitcast.72), kind=kLoop, calls=%fused_computation.29.clone.1 | loop fusion | flops 524288 | bytes 4200448 | tf_op jit(solution)/shard_map/while/body/eval_jaxpr/cos | solution.py:64
  136.2 2.8 %fusion.58 = f32[2048,64]{0,1:T(8,128)S(1)} fusion(f32[512,1024]{1,0:T(8,128)S(1)} %get-tuple-element.347, f32[512,1024]{1,0:T(8,128)S(1)} %get-tuple-element.348, f32[512,32]{0,1:T(8,128)S(1)} %get-tuple-element.352, f32[512,32]{0,1:T(8,128)S(1)} %get-tuple-element.353), kind=kOutput, calls=%fused_computation.24.clone.1 | convolution fusion | flops 806387712 | bytes 4849664 | tf_op jit(solution)/shard_map/while/body/eval_jaxpr/dot_general | solution.py:66
  139.6 7.3 %multiply_cosine_fusion.7 = (f32[512,1024]{1,0:T(8,128)S(1)}, f32[512,1024]{1,0:T(8,128)S(1)}) fusion(f32[1024]{0:T(1024)S(1)} %convert_add_fusion.6, f32[512]{0:T(512)S(1)} %bitcast.72), kind=kLoop, calls=%fused_computation.29.clone.1 | loop fusion | flops 524288 | bytes 4200448 | tf_op jit(solution)/shard_map/while/body/eval_jaxpr/cos | solution.py:64
  146.9 2.8 %fusion.58 = f32[2048,64]{0,1:T(8,128)S(1)} fusion(f32[512,1024]{1,0:T(8,128)S(1)} %get-tuple-element.347, f32[512,1024]{1,0:T(8,128)S(1)} %get-tuple-element.348, f32[512,32]{0,1:T(8,128)S(1)} %get-tuple-element.352, f32[512,32]{0,1:T(8,128)S(1)} %get-tuple-element.353), kind=kOutput, calls=%fused_computation.24.clone.1 | convolution fusion | flops 806387712 | bytes 4849664 | tf_op jit(solution)/shard_map/while/body/eval_jaxpr/dot_general | solution.py:66
  150.3 7.3 %multiply_cosine_fusion.7 = (f32[512,1024]{1,0:T(8,128)S(1)}, f32[512,1024]{1,0:T(8,128)S(1)}) fusion(f32[1024]{0:T(1024)S(1)} %convert_add_fusion.6, f32[512]{0:T(512)S(1)} %bitcast.72), kind=kLoop, calls=%fused_computation.29.clone.1 | loop fusion | flops 524288 | bytes 4200448 | tf_op jit(solution)/shard_map/while/body/eval_jaxpr/cos | solution.py:64
  157.6 2.8 %fusion.58 = f32[2048,64]{0,1:T(8,128)S(1)} fusion(f32[512,1024]{1,0:T(8,128)S(1)} %get-tuple-element.347, f32[512,1024]{1,0:T(8,128)S(1)} %get-tuple-element.348, f32[512,32]{0,1:T(8,128)S(1)} %get-tuple-element.352, f32[512,32]{0,1:T(8,128)S(1)} %get-tuple-element.353), kind=kOutput, calls=%fused_computation.24.clone.1 | convolution fusion | flops 806387712 | bytes 4849664 | tf_op jit(solution)/shard_map/while/body/eval_jaxpr/dot_general | solution.py:66
  161.0 7.3 %multiply_cosine_fusion.7 = (f32[512,1024]{1,0:T(8,128)S(1)}, f32[512,1024]{1,0:T(8,128)S(1)}) fusion(f32[1024]{0:T(1024)S(1)} %convert_add_fusion.6, f32[512]{0:T(512)S(1)} %bitcast.72), kind=kLoop, calls=%fused_computation.29.clone.1 | loop fusion | flops 524288 | bytes 4200448 | tf_op jit(solution)/shard_map/while/body/eval_jaxpr/cos | solution.py:64
  168.4 2.8 %fusion.58 = f32[2048,64]{0,1:T(8,128)S(1)} fusion(f32[512,1024]{1,0:T(8,128)S(1)} %get-tuple-element.347, f32[512,1024]{1,0:T(8,128)S(1)} %get-tuple-element.348, f32[512,32]{0,1:T(8,128)S(1)} %get-tuple-element.352, f32[512,32]{0,1:T(8,128)S(1)} %get-tuple-element.353), kind=kOutput, calls=%fused_computation.24.clone.1 | convolution fusion | flops 806387712 | bytes 4849664 | tf_op jit(solution)/shard_map/while/body/eval_jaxpr/dot_general | solution.py:66
  171.3 1.0 copy.26
  172.4 66.3 %reduce-scatter.4.cloned.1.call-done = f32[64,64]{1,0:T(8,128)} async-done(((f32[1024,64]{1,0:T(8,128)}), f32[64,64]{1,0:T(8,128)}) %reduce-scatter.4.cloned.1.call-update) | async-done | bytes 16400 | tf_op jit(solution)/shard_map/reduce_scatter | solution.py:138
  238.6 0.9 fusion.34
  (76 shorter events, 7.0 us)
Async XLA Ops:
  7.2 231.5 %reduce-scatter.4.cloned.1.call-start = ((), (), s32[]{:S(2)}) async-start(), calls=%async_computation.1 | async-start | bytes 557056 | tf_op jit(solution)/shard_map/reduce_scatter | solution.py:138
  8.2 42.6 %copy-start.2 = (s32[2048]{0:T(1024)S(1)}, s32[2048]{0:T(1024)}, u32[]{:S(2)}) copy-start(s32[2048]{0:T(1024)} %param.13) | copy-start | bytes 24580
  8.2 42.6 %copy-start.3 = (s32[2048]{0:T(1024)S(1)}, s32[2048]{0:T(1024)}, u32[]{:S(2)}) copy-start(s32[2048]{0:T(1024)} %param.12) | copy-start | bytes 24580
  8.3 42.6 %copy-start.5 = (s32[32]{0:T(128)S(1)}, s32[32]{0:T(128)}, u32[]{:S(2)}) copy-start(s32[32]{0:T(128)} %param.11) | copy-start | bytes 388
  51.2 76.6 %copy-start.1 = (f32[2,2048]{1,0:T(2,128)S(1)}, f32[2,2048]{1,0:T(2,128)}, u32[]{:S(2)}) copy-start(f32[2,2048]{1,0:T(2,128)} %param.14) | copy-start | bytes 49156
  51.2 76.7 %copy-start.4 = (f32[2048]{0:T(1024)S(1)}, f32[2048]{0:T(1024)}, u32[]{:S(2)}) copy-start(f32[2048]{0:T(1024)} %param.15) | copy-start | bytes 24580
  99.2 3.1 %collective-permute-start = (f32[2,2048]{1,0:T(2,128)S(1)}, f32[2,2048]{1,0:T(2,128)S(1)}, u32[]{:S(2)}, u32[]{:S(2)}) collective-permute-start(f32[2,2048]{1,0:T(2,128)S(1)} %bitcast.82), channel_id=1, source_target_pairs={{0,1},{1,0},{2,3},{3,2},{4,5},{5,4},{6,7},{7,6},{8,9},{9,8},{10,11... | collective-permute-start | bytes 49160 | tf_op jit(solution)/shard_map/ppermute | solution.py:18
  102.3 5.6 %collective-permute-start.1 = (f32[2,2048]{1,0:T(2,128)S(1)}, f32[2,2048]{1,0:T(2,128)S(1)}, u32[]{:S(2)}, u32[]{:S(2)}) collective-permute-start(f32[2,2048]{1,0:T(2,128)S(1)} %add.67), channel_id=1, source_target_pairs={{0,2},{1,3},{2,0},{3,1},{4,6},{5,7},{6,4},{7,5},{8,10},{9,11},{10,... | collective-permute-start | bytes 49160 | tf_op jit(solution)/shard_map/ppermute | solution.py:18
  107.9 7.1 %collective-permute-start.2 = (f32[2,2048]{1,0:T(2,128)S(1)}, f32[2,2048]{1,0:T(2,128)S(1)}, u32[]{:S(2)}, u32[]{:S(2)}) collective-permute-start(f32[2,2048]{1,0:T(2,128)S(1)} %add.68), channel_id=1, source_target_pairs={{0,4},{1,5},{2,6},{3,7},{4,0},{5,1},{6,2},{7,3},{8,12},{9,13},{10,... | collective-permute-start | bytes 49160 | tf_op jit(solution)/shard_map/ppermute | solution.py:18
  115.1 5.6 %collective-permute-start.3 = (f32[2,2048]{1,0:T(2,128)S(1)}, f32[2,2048]{1,0:T(2,128)S(1)}, u32[]{:S(2)}, u32[]{:S(2)}) collective-permute-start(f32[2,2048]{1,0:T(2,128)S(1)} %add.69), channel_id=1, source_target_pairs={{0,8},{1,9},{2,10},{3,11},{4,12},{5,13},{6,14},{7,15},{8,0},{9,1},... | collective-permute-start | bytes 49160 | tf_op jit(solution)/shard_map/ppermute | solution.py:18
  120.7 7.1 %collective-permute-start.4 = (f32[2,2048]{1,0:T(2,128)S(1)}, f32[2,2048]{1,0:T(2,128)S(1)}, u32[]{:S(2)}, u32[]{:S(2)}) collective-permute-start(f32[2,2048]{1,0:T(2,128)S(1)} %add.70), channel_id=1, source_target_pairs={{0,16},{1,17},{2,18},{3,19},{4,20},{5,21},{6,22},{7,23},{8,24},{9,... | collective-permute-start | bytes 49160 | tf_op jit(solution)/shard_map/ppermute | solution.py:18
  127.9 0.6 copy-start
Sparse Core Ops, SparseCore 0:
  172.5 66.1 reduce-scatter.3
